TPU v7x, 256 devices: a whole 4x4x8 slice. The times are simulated.
256 devices in a mesh: section: 2 (over y_hi), sx: 16 (over z, core), sy: 8 (over y_lo, x).
Axes of the slice: x: 4, y: 4 (y_hi: 2, y_lo: 2; y = y_hi * 2 + y_lo), z: 8, core: 2. Of those that a mesh axis runs over, the one named last changes fastest.
Arguments:
- previous: float32 [16, 256, 1024], P(None, 'sx', 'sy'), may hold values from -3 to 3
- sections: float32 [4, 16, 256, 1024], P('section', None, 'sx', 'sy'), may hold values from -3 to 3
- diffusivity: float32 [16, 256, 1024], P(None, 'sx', 'sy'), may hold values from 0.3 to 3
- reaction: float32 [16, 256, 1024], P(None, 'sx', 'sy'), may hold values from 0.2 to 2
Outputs:
- updated: float32 [4, 16, 256, 1024], P('section', None, 'sx', 'sy')
All inputs are finite; a program needn't handle non-finite values.
Results may differ from a plain program's by a relative error of at most 0.0003.
Values sent between devices are 32-bit elements; how exact they have to be, the bound alone decides.
No kernel may reach another device: no remote copies, remote signals or barrier semaphores. Data moves between devices by JAX's collectives and lax.ppermute only.
A program may use at most 64 MiB of HBM per device.

v0:
```python
import jax
import jax.numpy as jnp
from jax import lax
from jax.sharding import PartitionSpec as P

ITERS = 4
step_size = 1.0
tiny_value = 1e-06


def extended(cells, sides, width):
    for axis, dim in sides:
        count = lax.axis_size(axis)
        ends = count - 1
        head = lax.slice_in_dim(cells, 0, width, axis=dim)
        tail = lax.slice_in_dim(cells, cells.shape[dim] - width, cells.shape[dim], axis=dim)
        cells = jnp.concatenate(
            [
                lax.ppermute(tail, axis, [(i, (i + 1) % count) for i in range(ends)]),
                cells,
                lax.ppermute(head, axis, [((i + 1) % count, i) for i in range(ends)]),
            ],
            axis=dim,
        )
    return cells


def invert_table(matrix):
    order_n = len(matrix)
    augmented = [
        list(matrix[r]) + [1.0 if c == r else 0.0 for c in range(order_n)] for r in range(order_n)
    ]
    for col in range(order_n):
        pivot_row = max(range(col, order_n), key=lambda r: abs(augmented[r][col]))
        augmented[col], augmented[pivot_row] = (augmented[pivot_row], augmented[col])
        leading = augmented[col][col]
        augmented[col] = [v / leading for v in augmented[col]]
        for r in range(order_n):
            if r != col:
                factor = augmented[r][col]
                augmented[r] = [a - factor * b for a, b in zip(augmented[r], augmented[col])]
    return [row_values[order_n:] for row_values in augmented]


def table_product(left, right):
    return [
        [sum((left[i][k] * right[k][j] for k in range(len(right)))) for j in range(len(right[0]))]
        for i in range(len(left))
    ]


def pair_add(first, second):
    return (first[0] + second[0], first[1] + second[1])


def pair_sub(first, second):
    return (first[0] - second[0], first[1] - second[1])


def pair_mul(first, second):
    return (
        first[0] * second[0] - first[1] * second[1],
        first[0] * second[1] + first[1] * second[0],
    )


def pair_div(first, second):
    scale_sq = second[0] * second[0] + second[1] * second[1]
    return (
        (first[0] * second[0] + first[1] * second[1]) / scale_sq,
        (first[1] * second[0] - first[0] * second[1]) / scale_sq,
    )


def quartic_value(point):
    return (((210.0 * point - 480.0) * point + 360.0) * point - 96.0) * point + 6.0


def bisect_root(lower, upper):
    for count in range(200):
        middle = 0.5 * (lower + upper)
        if (quartic_value(lower) < 0.0) == (quartic_value(middle) < 0.0):
            lower = middle
        else:
            upper = middle
    return 0.5 * (lower + upper)


def radau_tables():
    abscissae = []
    grid_steps = 4000
    for m in range(grid_steps):
        lower = 0.999 * m / grid_steps
        upper = 0.999 * (m + 1) / grid_steps
        if (quartic_value(lower) < 0.0) != (quartic_value(upper) < 0.0):
            abscissae.append(bisect_root(lower, upper))
    abscissae.append(1.0)
    vander = [[abscissae[j] ** k for k in range(4)] for j in range(4)]
    moments = [[abscissae[i] ** (k + 1) / (k + 1) for k in range(4)] for i in range(4)]
    tableau = table_product(moments, invert_table(vander))
    inverse = invert_table(tableau)
    running = [list(row_values) for row_values in inverse]
    coeffs = []
    for k in range(1, 5):
        trace_value = sum((running[i][i] for i in range(4)))
        coeffs.append(-trace_value / k)
        shifted_table = [
            [running[i][j] + (coeffs[-1] if i == j else 0.0) for j in range(4)] for i in range(4)
        ]
        running = table_product(inverse, shifted_table)
    start_point = (0.4, 0.9)
    estimates = [(1.0, 0.0)]
    for k in range(3):
        estimates.append(pair_mul(estimates[-1], start_point))
    for count in range(500):
        for i in range(4):
            value = (1.0, 0.0)
            for coef_value in coeffs:
                value = pair_add(pair_mul(value, estimates[i]), (coef_value, 0.0))
            denom = (1.0, 0.0)
            for j in range(4):
                if j != i:
                    denom = pair_mul(denom, pair_sub(estimates[i], estimates[j]))
            estimates[i] = pair_sub(estimates[i], pair_div(value, denom))
    chosen = [m for m in range(4) if estimates[m][1] > 0.0]
    ranking = sorted(chosen, key=lambda m: -estimates[m][1])
    columns = []
    pairs = []
    for m in ranking:
        eigen_pair = estimates[m]
        system = [
            [
                (
                    inverse[i][j] - (eigen_pair[0] if i == j else 0.0),
                    -(eigen_pair[1] if i == j else 0.0),
                )
                for j in range(4)
            ]
            for i in range(3)
        ]
        rows_left = [
            [system[i][j] for j in range(3)] + [(-system[i][3][0], -system[i][3][1])]
            for i in range(3)
        ]
        for col in range(3):
            pivot_row = max(
                range(col, 3), key=lambda r: rows_left[r][col][0] ** 2 + rows_left[r][col][1] ** 2
            )
            rows_left[col], rows_left[pivot_row] = (rows_left[pivot_row], rows_left[col])
            leading = rows_left[col][col]
            rows_left[col] = [pair_div(v, leading) for v in rows_left[col]]
            for r in range(3):
                if r != col:
                    factor = rows_left[r][col]
                    rows_left[r] = [
                        pair_sub(a, pair_mul(factor, b))
                        for a, b in zip(rows_left[r], rows_left[col])
                    ]
        vector = [rows_left[i][3] for i in range(3)] + [(1.0, 0.0)]
        columns.append([v[0] for v in vector])
        columns.append([v[1] for v in vector])
        pairs.append((eigen_pair[0], eigen_pair[1]))
    eigen_basis = [[columns[j][i] for j in range(4)] for i in range(4)]
    basis_inverse = invert_table(eigen_basis)
    return (tableau, inverse, eigen_basis, basis_inverse, pairs)


def center(padded):
    return padded[..., 1:-1, 1:-1, 1:-1]


def shifted(padded, member):
    if member == 0:
        return padded[..., 2:, 1:-1, 1:-1]
    if member == 1:
        return padded[..., :-2, 1:-1, 1:-1]
    if member == 2:
        return padded[..., 1:-1, 2:, 1:-1]
    if member == 3:
        return padded[..., 1:-1, :-2, 1:-1]
    if member == 4:
        return padded[..., 1:-1, 1:-1, 2:]
    return padded[..., 1:-1, 1:-1, :-2]


def face_terms(padded):
    middle = center(padded)
    return [0.5 * (middle + shifted(padded, m)) for m in range(6)]


def face_total(faces):
    total = faces[0]
    for m in range(1, 6):
        total = total + faces[m]
    return total


def neighbour_sum(faces, padded):
    total = faces[0] * shifted(padded, 0)
    for m in range(1, 6):
        total = total + faces[m] * shifted(padded, m)
    return total


def pad_depth(field, width):
    return jnp.pad(field, [(0, 0)] * (field.ndim - 3) + [(width, width), (0, 0), (0, 0)])


def trim_cells(field, width):
    if width == 0:
        return field
    return field[..., width:-width, width:-width, width:-width]


def apply_inverse(diag_real, coupling, determinant, vector):
    first = (diag_real * vector[0] - coupling * vector[1]) / determinant
    second = (coupling * vector[0] + diag_real * vector[1]) / determinant
    return jnp.stack([first, second])


def apply_block(diag_real, coupling, vector):
    return jnp.stack(
        [diag_real * vector[0] + coupling * vector[1], diag_real * vector[1] - coupling * vector[0]]
    )


def combine(coef, fields):
    total = coef[:, 0][:, None, None, None] * fields[0][None]
    for column in range(1, fields.shape[0]):
        total = total + coef[:, column][:, None, None, None] * fields[column][None]
    return total


def body(previous, sections, diffusivity, reaction):
    tableau, inverse, eigen_basis, basis_inverse, pairs = radau_tables()
    flux_rows = jnp.asarray(basis_inverse, jnp.float32)
    shift_table = table_product(basis_inverse, inverse)
    shift_rows = jnp.asarray(
        [[v / step_size for v in row_values] for row_values in shift_table], jnp.float32
    )
    basis_rows = jnp.asarray(eigen_basis, jnp.float32)
    pair_table = jnp.asarray([list(p) for p in pairs], jnp.float32)
    eigen_block = lax.axis_index("section")
    section_coef = diffusivity * (1.0 + 0.5 * jnp.tanh(sections))
    frozen_coef = diffusivity * (1.0 + 0.5 * jnp.tanh(previous))
    react_slope = reaction * (1.0 - 3.0 * previous * previous)
    coefs = jnp.concatenate([section_coef, frozen_coef[None], react_slope[None]], 0)
    halo_width = 1
    section_pad, coef_pad = (
        extended(sections, (("sx", 2), ("sy", 3)), halo_width),
        extended(coefs, (("sx", 2), ("sy", 3)), halo_width),
    )
    section_pad = pad_depth(section_pad, halo_width)
    coef_pad = pad_depth(coef_pad, halo_width)
    section_near = trim_cells(section_pad, halo_width - 1)
    coef_near = trim_cells(coef_pad, halo_width - 1)
    section_faces = face_terms(coef_near[:2])
    section_flux = neighbour_sum(section_faces, section_near) - face_total(section_faces) * sections
    section_flux = section_flux + reaction * sections * (1.0 - sections * sections)
    increment = sections - previous
    all_flux, all_increment = (
        lax.all_gather(section_flux, "section", axis=0, tiled=True),
        lax.all_gather(increment, "section", axis=0, tiled=True),
    )
    own_flux = lax.dynamic_slice(flux_rows, (2 * eigen_block, 0), (2, 4))
    own_shift = lax.dynamic_slice(shift_rows, (2 * eigen_block, 0), (2, 4))
    rhs = combine(own_flux, all_flux) - combine(own_shift, all_increment)
    faces_region = face_terms(coef_pad[2])
    slope_region = trim_cells(coef_pad[3], 1)
    real_part = pair_table[eigen_block, 0] / step_size
    coupling = pair_table[eigen_block, 1] / step_size
    diag_region = real_part + face_total(faces_region) - slope_region
    det_region = diag_region * diag_region + coupling * coupling
    inner_cut = halo_width - 1
    faces_inner = [trim_cells(face, inner_cut) for face in faces_region]
    diag_inner = trim_cells(diag_region, inner_cut)
    det_inner = trim_cells(det_region, inner_cut)
    residue = rhs
    correction = jnp.zeros_like(residue)
    for sweep in range(ITERS):
        scaled = apply_inverse(diag_inner, coupling, det_inner, residue)
        scaled_pad = extended(scaled, (("sx", 2), ("sy", 3)), halo_width)
        scaled_pad = pad_depth(scaled_pad, halo_width)
        search = scaled + apply_inverse(
            diag_inner, coupling, det_inner, neighbour_sum(faces_inner, scaled_pad)
        )
        search_pad = extended(search, (("sx", 2), ("sy", 3)), 1)
        search_pad = pad_depth(search_pad, 1)
        image = apply_block(diag_inner, coupling, search) - neighbour_sum(faces_inner, search_pad)
        numerator, denominator = lax.psum(
            (jnp.sum(image * residue), jnp.sum(image * image)), ("sx", "sy")
        )
        step_length = numerator / (denominator + tiny_value)
        correction = correction + step_length * search
        residue = residue - step_length * image
    gathered = lax.all_gather(correction, "section", axis=0, tiled=True)
    own_basis = lax.dynamic_slice(basis_rows, (2 * eigen_block, 0), (2, 4))
    return sections + combine(own_basis, gathered)


def solution(mesh):
    in_specs = (
        P(None, "sx", "sy"),
        P("section", None, "sx", "sy"),
        P(None, "sx", "sy"),
        P(None, "sx", "sy"),
    )
    out_specs = P("section", None, "sx", "sy")
    return jax.shard_map(body, mesh=mesh, in_specs=in_specs, out_specs=out_specs, check_vma=False)
```

profile of v0, /device:TPU:130, one launch (start us, length us, event | category | flops | bytes accessed | tf_op | source)
XLA Modules:
  0.0 1369.5 jit_solution(1758878238142489170)
XLA Ops:
  1.8 1.9 collective-permute-start.4
  3.7 4.9 collective-permute-start.5
  10.4 8.7 all_gather.10
  24.3 1.9 collective-permute-start
  26.2 4.9 collective-permute-start.1
  31.2 3.4 collective-permute-start.6
  34.6 3.1 collective-permute-start.7
  38.6 2.7 collective-permute-start.2
  41.8 3.1 collective-permute-start.3
  52.7 8.6 all_gather.9
  64.2 1.9 collective-permute-start.8
  66.1 4.9 collective-permute-start.9
  72.6 4.7 collective-permute-start.10
  77.3 1.9 collective-permute-start.11
  79.2 3.2 collective-permute-done.10
  82.4 6.5 collective-permute-done.11
  90.6 1.9 collective-permute-start.12
  92.5 4.9 collective-permute-start.13
  99.0 3.6 collective-permute-start.14
  102.6 2.2 collective-permute-start.15
  105.6 3.8 collective-permute-done.14
  109.4 4.3 collective-permute-done.15
  114.1 2.0 multiply_reduce_fusion.6
  116.1 276.0 %all-reduce.13 = (f32[]{:T(128)}, f32[]{:T(128)}) all-reduce(f32[]{:T(128)} %get-tuple-element.12, f32[]{:T(128)} %get-tuple-element.11), channel_id=1, replica_groups=mesh['section'=2,'sx'=16,'sy'=8] {'sx','sy'}, use_global_device_ids=true, to_apply=%region_1.2 | all-reduce | flops 2 | bytes 16 | tf_op jit(solution)/shard_map/psum | solution.py:290
  395.3 1.9 collective-permute-start.16
  397.2 4.9 collective-permute-start.17
  403.6 1.9 collective-permute-start.18
  405.6 3.9 collective-permute-start.19
  409.5 2.7 collective-permute-done.18
  412.3 1.9 collective-permute-done.19
  415.8 1.9 collective-permute-start.20
  417.8 4.9 collective-permute-start.21
  424.2 1.9 collective-permute-start.22
  426.2 4.1 collective-permute-start.23
  431.0 1.8 collective-permute-done.22
  432.8 1.9 collective-permute-done.23
  436.3 278.6 %all-reduce.12 = (f32[]{:T(128)}, f32[]{:T(128)}) all-reduce(f32[]{:T(128)} %get-tuple-element.10, f32[]{:T(128)} %get-tuple-element.9), channel_id=1, replica_groups=mesh['section'=2,'sx'=16,'sy'=8] {'sx','sy'}, use_global_device_ids=true, to_apply=%region_5.6 | all-reduce | flops 2 | bytes 16 | tf_op jit(solution)/shard_map/psum | solution.py:290
  717.0 1.9 collective-permute-start.24
  719.0 4.9 collective-permute-start.25
  725.4 1.9 collective-permute-start.26
  727.3 3.9 collective-permute-start.27
  731.3 2.7 collective-permute-done.26
  734.0 1.9 collective-permute-done.27
  737.6 1.9 collective-permute-start.28
  739.6 4.9 collective-permute-start.29
  746.0 1.9 collective-permute-start.30
  747.9 3.9 collective-permute-start.31
  752.6 2.0 collective-permute-done.30
  754.6 1.9 collective-permute-done.31
  758.1 278.6 %all-reduce.11 = (f32[]{:T(128)}, f32[]{:T(128)}) all-reduce(f32[]{:T(128)} %get-tuple-element.8, f32[]{:T(128)} %get-tuple-element.7), channel_id=1, replica_groups=mesh['section'=2,'sx'=16,'sy'=8] {'sx','sy'}, use_global_device_ids=true, to_apply=%region_9.10 | all-reduce | flops 2 | bytes 16 | tf_op jit(solution)/shard_map/psum | solution.py:290
  1038.8 1.9 collective-permute-start.32
  1040.7 4.9 collective-permute-start.33
  1047.1 1.9 collective-permute-start.34
  1049.1 3.9 collective-permute-start.35
  1053.1 2.7 collective-permute-done.34
  1055.8 1.9 collective-permute-done.35
  1059.4 1.9 collective-permute-start.36
  1061.3 4.9 collective-permute-start.37
  1067.7 1.9 collective-permute-start.38
  1069.7 3.9 collective-permute-start.39
  1074.3 2.0 collective-permute-done.38
  1076.4 1.9 collective-permute-done.39
  1079.8 278.7 %all-reduce.10 = (f32[]{:T(128)}, f32[]{:T(128)}) all-reduce(f32[]{:T(128)} %get-tuple-element.6, f32[]{:T(128)} %get-tuple-element.5), channel_id=1, replica_groups=mesh['section'=2,'sx'=16,'sy'=8] {'sx','sy'}, use_global_device_ids=true, to_apply=%region_13.14 | all-reduce | flops 2 | bytes 16 | tf_op jit(solution)/shard_map/psum | solution.py:290
  1360.0 8.6 all_gather.11
  (158 shorter events, 50.8 us)
Async XLA Ops:
  0.0 19.2 %copy-start.7 = (f32[16,16,128]{2,1,0:T(8,128)S(1)}, f32[16,16,128]{2,1,0:T(8,128)}, u32[]{:S(2)}) copy-start(f32[16,16,128]{2,1,0:T(8,128)} %param.8) | copy-start | bytes 393220
  0.0 19.2 %copy-start.10 = (f32[16,16,128]{2,1,0:T(8,128)S(1)}, f32[16,16,128]{2,1,0:T(8,128)}, u32[]{:S(2)}) copy-start(f32[16,16,128]{2,1,0:T(8,128)} %param.10) | copy-start | bytes 393220
  0.0 19.2 %copy-start.9 = (f32[16,16,128]{2,1,0:T(8,128)S(1)}, f32[16,16,128]{2,1,0:T(8,128)}, u32[]{:S(2)}) copy-start(f32[16,16,128]{2,1,0:T(8,128)} %param.11) | copy-start | bytes 393220
  1.1 0.7 copy-start.3
  1.8 22.3 %collective-permute-start.4 = (f32[2,16,1,128]{3,1,2,0:T(8,128)S(1)}, f32[2,16,1,128]{3,1,2,0:T(8,128)S(1)}, u32[]{:S(2)}, u32[]{:S(2)}) collective-permute-start(f32[2,16,1,128]{3,1,2,0:T(8,128)S(1)} %get-tuple-element.109), channel_id=1, source_target_pairs={{0,8},{8,16},{16,24},{24,32},{32,40},{40,48},{48,56},{56,64},{64,7... | collective-permute-start | bytes 49160 | tf_op jit(solution)/shard_map/ppermute | solution.py:19
  3.7 27.3 %collective-permute-start.5 = (f32[2,16,1,128]{3,1,2,0:T(8,128)S(1)}, f32[2,16,1,128]{3,1,2,0:T(8,128)S(1)}, u32[]{:S(2)}, u32[]{:S(2)}) collective-permute-start(f32[2,16,1,128]{3,1,2,0:T(8,128)S(1)} %get-tuple-element.108), channel_id=1, source_target_pairs={{8,0},{16,8},{24,16},{32,24},{40,32},{48,40},{56,48},{64,56},{72,6... | collective-permute-start | bytes 49160 | tf_op jit(solution)/shard_map/ppermute | solution.py:21
  10.4 11.7 copy-start.16
  10.4 13.7 %copy-start = (f32[2,16,16,128]{3,2,1,0:T(8,128)S(1)}, f32[2,16,16,128]{3,2,1,0:T(8,128)}, u32[]{:S(2)}) copy-start(f32[2,16,16,128]{3,2,1,0:T(8,128)} %param.9) | copy-start | bytes 786436
  24.3 13.5 collective-permute-start
  26.2 11.6 collective-permute-start.1
  31.2 13.7 collective-permute-start.6
  34.6 10.3 collective-permute-start.7
  38.6 7.8 collective-permute-start.2
  41.8 5.9 collective-permute-start.3
  49.8 1.0 copy-start.4
  49.8 1.0 copy-start.8
  52.6 9.0 copy-start.1
  52.6 9.0 copy-start.2
  52.6 9.0 copy-start.11
  52.6 9.0 copy-start.12
  52.6 9.0 copy-start.13
  52.6 9.0 copy-start.14
  64.2 6.8 collective-permute-start.8
  66.1 6.3 collective-permute-start.9
  72.6 9.8 collective-permute-start.10
  77.3 11.6 collective-permute-start.11
  90.5 8.5 copy-start.5
  90.6 6.8 collective-permute-start.12
  92.5 6.3 collective-permute-start.13
  99.0 10.4 collective-permute-start.14
  102.6 11.1 collective-permute-start.15
  395.3 6.8 collective-permute-start.16
  397.2 6.3 collective-permute-start.17
  403.6 8.6 collective-permute-start.18
  405.6 8.6 collective-permute-start.19
  415.8 6.8 collective-permute-start.20
  417.8 6.3 collective-permute-start.21
  424.2 8.6 collective-permute-start.22
  426.2 8.6 collective-permute-start.23
  717.0 6.8 collective-permute-start.24
  719.0 6.3 collective-permute-start.25
  725.4 8.6 collective-permute-start.26
  727.3 8.6 collective-permute-start.27
  737.6 6.8 collective-permute-start.28
  739.6 6.3 collective-permute-start.29
  746.0 8.6 collective-permute-start.30
  747.9 8.6 collective-permute-start.31
  758.1 295.0 %copy-start.15 = (f32[4,4]{0,1:T(4,128)S(1)}, f32[4,4]{0,1:T(4,128)}, u32[]{:S(2)}) copy-start(f32[4,4]{0,1:T(4,128)} %constant.38.clone) | copy-start | bytes 196
  1038.8 6.8 collective-permute-start.32
  1040.7 6.3 collective-permute-start.33
  1047.1 8.6 collective-permute-start.34
  1049.1 8.6 collective-permute-start.35
  1059.4 6.8 collective-permute-start.36
  1061.3 6.3 collective-permute-start.37
  1067.7 8.6 collective-permute-start.38
  1069.7 8.6 collective-permute-start.39
  1078.7 281.1 %copy-start.6 = (f32[1,16,16,128]{3,1,2,0:T(8,128)S(1)}, f32[1,16,16,128]{3,1,2,0:T(8,128)}, u32[]{:S(2)}) copy-start(f32[1,16,16,128]{3,1,2,0:T(8,128)} %copy-done.5) | copy-start | bytes 393220
where the time goes:
time: 1370 us
  blocking collectives  1140 us (83%)
  starting transfers between devices  128 us (9%)
  waiting for transfers between devices  55.5 us (4%)
  other arithmetic  29.6 us (2%)
    psum x4, blocking collectives, body(): lax.psum((jnp.sum(image * residue), jnp.sum(image * image)), ('sx', 'sy'))  1110 us
    ppermute x20, starting transfers between devices, extended(): lax.ppermute(head, axis, [((i + 1) % count, i) for i in range(ends)])  82.7 us
    ppermute x20, starting transfers between devices, extended(): lax.ppermute(tail, axis, [(i, (i + 1) % count) for i in range(ends)])  45.1 us
    ppermute x20, waiting for transfers between devices, extended(): lax.ppermute(head, axis, [((i + 1) % count, i) for i in range(ends)])  34.4 us
  transfers between devices with their start and end apart: 40, of which 25 were waited for; matrix products, arithmetic and copies ran while one was open for 1% of the time, Pallas kernels for 0%

commit v1 on v0

--- a/solution.py
+++ b/solution.py
@@ -288,7 +288,7 @@
         search_pad = pad_depth(search_pad, 1)
         image = apply_block(diag_inner, coupling, search) - neighbour_sum(faces_inner, search_pad)
         numerator, denominator = lax.psum(
-            (jnp.sum(image * residue), jnp.sum(image * image)), ("sx", "sy")
+            lax.psum((jnp.sum(image * residue), jnp.sum(image * image)), "sx"), "sy"
         )
         step_length = numerator / (denominator + tiny_value)
         correction = correction + step_length * search

time: 1370 us -> 457 us (0.33)
  blocking collectives: 1140 us -> 195 us
  waiting for transfers between devices: 55.5 us -> 74.4 us
    psum x4 -> x8, blocking collectives: 1110 us -> 170 us  [the longest x4 104 us: body(): lax.psum((jnp.sum(image * residue), jnp.sum(image * image)), 'sx')]
    ppermute x20, waiting for transfers between devices: 34.4 us -> 54.5 us  [extended(): lax.ppermute(head, axis, [((i + 1) % count, i) for i in range(ends)])]
    ppermute x20, starting transfers between devices: 45.1 us -> 64.1 us  [extended(): lax.ppermute(tail, axis, [(i, (i + 1) % count) for i in range(ends)])]
  transfers between devices with their start and end apart: 40 -> 40, of which waited for: 25 -> 25; matrix products, arithmetic and copies ran while one was open for 1% -> 2% of each run, Pallas kernels for 0% -> 0%
where the time goes in v1:
time: 457 us; the launch traced here: 451 us
  blocking collectives  195 us (43%)
  starting transfers between devices  135 us (30%)
  waiting for transfers between devices  74.4 us (16%)
  other arithmetic  28 us (6%)
  local copies, waits for them, and re-layouts  11 us (2%)
  between operations  7.25 us (2%)
    psum x4, blocking collectives, body(): lax.psum((jnp.sum(image * residue), jnp.sum(image * image)), 'sx')  104 us
    ppermute x20, starting transfers between devices, extended(): lax.ppermute(head, axis, [((i + 1) % count, i) for i in range(ends)])  70.7 us
    psum x4, blocking collectives, body(): lax.psum(lax.psum((jnp.sum(image * residue), jnp.sum(image * image)), 'sx...  66 us
    ppermute x20, starting transfers between devices, extended(): lax.ppermute(tail, axis, [(i, (i + 1) % count) for i in range(ends)])  64.1 us
    ppermute x20, waiting for transfers between devices, extended(): lax.ppermute(head, axis, [((i + 1) % count, i) for i in range(ends)])  54.5 us
    ppermute x20, waiting for transfers between devices, extended(): lax.ppermute(tail, axis, [(i, (i + 1) % count) for i in range(ends)])  19.9 us
  transfers between devices with their start and end apart: 40, of which 25 were waited for; matrix products, arithmetic and copies ran while one was open for 2% of the time, Pallas kernels for 0%

profile of v1, /device:TPU:130, one launch (start us, length us, event | category | flops | bytes accessed | tf_op | source)
XLA Modules:
  0.0 450.8 jit_solution(10455792952849505930)
XLA Ops:
  3.7 4.9 %collective-permute-start.5 = (f32[2,16,1,128]{3,1,2,0:T(8,128)S(1)}, f32[2,16,1,128]{3,1,2,0:T(8,128)S(1)}, u32[]{:S(2)}, u32[]{:S(2)}) collective-permute-start(f32[2,16,1,128]{3,1,2,0:T(8,128)S(1)} %get-tuple-element.116), channel_id=1, source_target_pairs={{8,0},{16,8},{24,16},{32,24},{40,32},{48,40},{56,48},{64,56},{72,6... | collective-permute-start | bytes 49160 | tf_op jit(solution)/shard_map/ppermute | solution.py:21
  10.4 8.7 %all_gather.10 = f32[4,16,16,128]{3,2,1,0:T(8,128)S(1)} all-gather(f32[2,16,16,128]{3,2,1,0:T(8,128)S(1)} %broadcast_subtract_fusion), channel_id=1, replica_groups=mesh['section'=2,'sx'=16,'sy'=8] {'section'}, dimensions={0}, use_global_device_ids=true | all-gather | bytes 786432 | tf_op jit(solution)/shard_map/all_gather | solution.py:263
  23.9 1.9 collective-permute-start
  25.8 4.9 %collective-permute-start.1 = (f32[4,16,1,128]{3,1,2,0:T(8,128)S(1)}, f32[4,16,1,128]{3,1,2,0:T(8,128)S(1)}, u32[]{:S(2)}, u32[]{:S(2)}) collective-permute-start(f32[4,16,1,128]{3,1,2,0:T(8,128)S(1)} %get-tuple-element.53), channel_id=1, source_target_pairs={{8,0},{16,8},{24,16},{32,24},{40,32},{48,40},{56,48},{64,56},{72,6... | collective-permute-start | bytes 98312 | tf_op jit(solution)/shard_map/ppermute | solution.py:21
  30.9 3.4 collective-permute-start.6
  34.3 3.1 collective-permute-start.7
  38.2 2.7 collective-permute-start.2
  41.4 3.1 collective-permute-start.3
  52.4 8.6 %all_gather.9 = f32[4,16,16,128]{3,2,1,0:T(8,128)S(1)} all-gather(f32[2,16,16,128]{3,2,1,0:T(8,128)S(1)} %copy.337), channel_id=1, replica_groups=mesh['section'=2,'sx'=16,'sy'=8] {'section'}, dimensions={0}, use_global_device_ids=true | all-gather | bytes 786432 | tf_op jit(solution)/shard_map/all_gather | solution.py:262
  63.6 1.9 collective-permute-start.8
  65.5 4.9 %collective-permute-start.9 = (f32[2,16,1,128]{3,1,2,0:T(8,128)S(1)}, f32[2,16,1,128]{3,1,2,0:T(8,128)S(1)}, u32[]{:S(2)}, u32[]{:S(2)}) collective-permute-start(f32[2,16,1,128]{3,1,2,0:T(8,128)S(1)} %get-tuple-element.113), channel_id=1, source_target_pairs={{8,0},{16,8},{24,16},{32,24},{40,32},{48,40},{56,48},{64,56},{72,6... | collective-permute-start | bytes 49160 | tf_op jit(solution)/shard_map/ppermute | solution.py:21
  71.9 4.7 %collective-permute-start.10 = (f32[2,16,18,1]{3,1,2,0:T(8,128)S(1)}, f32[2,16,18,1]{3,1,2,0:T(8,128)S(1)}, u32[]{:S(2)}, u32[]{:S(2)}) collective-permute-start(f32[2,16,18,1]{3,1,2,0:T(8,128)S(1)} %get-tuple-element.95), channel_id=1, source_target_pairs={{0,1},{1,2},{2,3},{3,4},{4,5},{5,6},{6,7},{8,9},{9,10},{10,11},{11... | collective-permute-start | bytes 6920 | tf_op jit(solution)/shard_map/ppermute | solution.py:19
  76.7 1.9 collective-permute-start.11
  78.6 3.2 collective-permute-done.10
  81.7 6.5 %collective-permute-done.11 = f32[2,16,18,1]{3,1,2,0:T(8,128)S(1)} collective-permute-done((f32[2,16,18,1]{3,1,2,0:T(8,128)S(1)}, f32[2,16,18,1]{3,1,2,0:T(8,128)S(1)}, u32[]{:S(2)}, u32[]{:S(2)}) %collective-permute-start.11) | collective-permute-done | bytes 2336 | tf_op jit(solution)/shard_map/ppermute | solution.py:21
  89.8 1.9 collective-permute-start.12
  91.7 4.9 %collective-permute-start.13 = (f32[2,16,1,128]{3,1,2,0:T(8,128)S(1)}, f32[2,16,1,128]{3,1,2,0:T(8,128)S(1)}, u32[]{:S(2)}, u32[]{:S(2)}) collective-permute-start(f32[2,16,1,128]{3,1,2,0:T(8,128)S(1)} %get-tuple-element.111), channel_id=1, source_target_pairs={{8,0},{16,8},{24,16},{32,24},{40,32},{48,40},{56,48},{64,56},{72,6... | collective-permute-start | bytes 49160 | tf_op jit(solution)/shard_map/ppermute | solution.py:21
  98.2 3.6 collective-permute-start.14
  101.9 2.2 collective-permute-start.15
  104.7 4.0 collective-permute-done.14
  108.6 4.3 collective-permute-done.15
  113.4 1.9 multiply_reduce_fusion.6
  115.3 24.3 %all-reduce.13 = (f32[]{:T(128)}, f32[]{:T(128)}) all-reduce(f32[]{:T(128)} %get-tuple-element.12, f32[]{:T(128)} %get-tuple-element.11), channel_id=1, replica_groups=mesh['section'=2,'sx'=16,'sy'=8] {'sx'}, use_global_device_ids=true, to_apply=%region_1.2 | all-reduce | flops 2 | bytes 16 | tf_op jit(solution)/shard_map/psum | solution.py:291
  139.6 16.5 %all-reduce.17 = (f32[]{:T(128)}, f32[]{:T(128)}) all-reduce(f32[]{:T(128)} %get-tuple-element.19, f32[]{:T(128)} %get-tuple-element.20), channel_id=1, replica_groups=mesh['section'=2,'sx'=16,'sy'=8] {'sy'}, use_global_device_ids=true, to_apply=%region_2.3 | all-reduce | flops 2 | bytes 16 | tf_op jit(solution)/shard_map/psum | solution.py:290
  159.1 1.9 collective-permute-start.16
  161.0 4.9 %collective-permute-start.17 = (f32[2,16,1,128]{3,1,2,0:T(8,128)S(1)}, f32[2,16,1,128]{3,1,2,0:T(8,128)S(1)}, u32[]{:S(2)}, u32[]{:S(2)}) collective-permute-start(f32[2,16,1,128]{3,1,2,0:T(8,128)S(1)} %get-tuple-element.109), channel_id=1, source_target_pairs={{8,0},{16,8},{24,16},{32,24},{40,32},{48,40},{56,48},{64,56},{72,6... | collective-permute-start | bytes 49160 | tf_op jit(solution)/shard_map/ppermute | solution.py:21
  167.5 4.0 collective-permute-start.18
  171.5 1.9 collective-permute-start.19
  173.5 2.7 collective-permute-done.18
  176.1 4.0 collective-permute-done.19
  181.7 1.9 collective-permute-start.20
  183.6 4.9 %collective-permute-start.21 = (f32[2,16,1,128]{3,1,2,0:T(8,128)S(1)}, f32[2,16,1,128]{3,1,2,0:T(8,128)S(1)}, u32[]{:S(2)}, u32[]{:S(2)}) collective-permute-start(f32[2,16,1,128]{3,1,2,0:T(8,128)S(1)} %get-tuple-element.107), channel_id=1, source_target_pairs={{8,0},{16,8},{24,16},{32,24},{40,32},{48,40},{56,48},{64,56},{72,6... | collective-permute-start | bytes 49160 | tf_op jit(solution)/shard_map/ppermute | solution.py:21
  190.1 6.1 %collective-permute-start.22 = (f32[2,16,18,1]{3,1,2,0:T(8,128)S(1)}, f32[2,16,18,1]{3,1,2,0:T(8,128)S(1)}, u32[]{:S(2)}, u32[]{:S(2)}) collective-permute-start(f32[2,16,18,1]{3,1,2,0:T(8,128)S(1)} %get-tuple-element.89), channel_id=1, source_target_pairs={{0,1},{1,2},{2,3},{3,4},{4,5},{5,6},{6,7},{8,9},{9,10},{10,11},{11... | collective-permute-start | bytes 6920 | tf_op jit(solution)/shard_map/ppermute | solution.py:19
  196.2 2.1 collective-permute-start.23
  200.4 6.5 %collective-permute-done.23 = f32[2,16,18,1]{3,1,2,0:T(8,128)S(1)} collective-permute-done((f32[2,16,18,1]{3,1,2,0:T(8,128)S(1)}, f32[2,16,18,1]{3,1,2,0:T(8,128)S(1)}, u32[]{:S(2)}, u32[]{:S(2)}) %collective-permute-start.23) | collective-permute-done | bytes 2336 | tf_op jit(solution)/shard_map/ppermute | solution.py:21
  208.5 26.4 %all-reduce.12 = (f32[]{:T(128)}, f32[]{:T(128)}) all-reduce(f32[]{:T(128)} %get-tuple-element.10, f32[]{:T(128)} %get-tuple-element.9), channel_id=1, replica_groups=mesh['section'=2,'sx'=16,'sy'=8] {'sx'}, use_global_device_ids=true, to_apply=%region_7.8 | all-reduce | flops 2 | bytes 16 | tf_op jit(solution)/shard_map/psum | solution.py:291
  234.9 16.5 %all-reduce.16 = (f32[]{:T(128)}, f32[]{:T(128)}) all-reduce(f32[]{:T(128)} %get-tuple-element.17, f32[]{:T(128)} %get-tuple-element.18), channel_id=1, replica_groups=mesh['section'=2,'sx'=16,'sy'=8] {'sy'}, use_global_device_ids=true, to_apply=%region_8.9 | all-reduce | flops 2 | bytes 16 | tf_op jit(solution)/shard_map/psum | solution.py:290
  253.3 1.9 collective-permute-start.24
  255.3 4.9 %collective-permute-start.25 = (f32[2,16,1,128]{3,1,2,0:T(8,128)S(1)}, f32[2,16,1,128]{3,1,2,0:T(8,128)S(1)}, u32[]{:S(2)}, u32[]{:S(2)}) collective-permute-start(f32[2,16,1,128]{3,1,2,0:T(8,128)S(1)} %get-tuple-element.105), channel_id=1, source_target_pairs={{8,0},{16,8},{24,16},{32,24},{40,32},{48,40},{56,48},{64,56},{72,6... | collective-permute-start | bytes 49160 | tf_op jit(solution)/shard_map/ppermute | solution.py:21
  261.7 4.0 collective-permute-start.26
  265.8 1.9 collective-permute-start.27
  267.7 2.7 collective-permute-done.26
  270.3 4.0 collective-permute-done.27
  275.9 1.9 collective-permute-start.28
  277.8 4.9 %collective-permute-start.29 = (f32[2,16,1,128]{3,1,2,0:T(8,128)S(1)}, f32[2,16,1,128]{3,1,2,0:T(8,128)S(1)}, u32[]{:S(2)}, u32[]{:S(2)}) collective-permute-start(f32[2,16,1,128]{3,1,2,0:T(8,128)S(1)} %get-tuple-element.103), channel_id=1, source_target_pairs={{8,0},{16,8},{24,16},{32,24},{40,32},{48,40},{56,48},{64,56},{72,6... | collective-permute-start | bytes 49160 | tf_op jit(solution)/shard_map/ppermute | solution.py:21
  284.3 6.1 %collective-permute-start.30 = (f32[2,16,18,1]{3,1,2,0:T(8,128)S(1)}, f32[2,16,18,1]{3,1,2,0:T(8,128)S(1)}, u32[]{:S(2)}, u32[]{:S(2)}) collective-permute-start(f32[2,16,18,1]{3,1,2,0:T(8,128)S(1)} %get-tuple-element.85), channel_id=1, source_target_pairs={{0,1},{1,2},{2,3},{3,4},{4,5},{5,6},{6,7},{8,9},{9,10},{10,11},{11... | collective-permute-start | bytes 6920 | tf_op jit(solution)/shard_map/ppermute | solution.py:19
  290.4 1.9 collective-permute-start.31
  294.7 6.5 %collective-permute-done.31 = f32[2,16,18,1]{3,1,2,0:T(8,128)S(1)} collective-permute-done((f32[2,16,18,1]{3,1,2,0:T(8,128)S(1)}, f32[2,16,18,1]{3,1,2,0:T(8,128)S(1)}, u32[]{:S(2)}, u32[]{:S(2)}) %collective-permute-start.31) | collective-permute-done | bytes 2336 | tf_op jit(solution)/shard_map/ppermute | solution.py:21
  302.7 26.4 %all-reduce.11 = (f32[]{:T(128)}, f32[]{:T(128)}) all-reduce(f32[]{:T(128)} %get-tuple-element.8, f32[]{:T(128)} %get-tuple-element.7), channel_id=1, replica_groups=mesh['section'=2,'sx'=16,'sy'=8] {'sx'}, use_global_device_ids=true, to_apply=%region_13.14 | all-reduce | flops 2 | bytes 16 | tf_op jit(solution)/shard_map/psum | solution.py:291
  329.1 16.5 %all-reduce.15 = (f32[]{:T(128)}, f32[]{:T(128)}) all-reduce(f32[]{:T(128)} %get-tuple-element.15, f32[]{:T(128)} %get-tuple-element.16), channel_id=1, replica_groups=mesh['section'=2,'sx'=16,'sy'=8] {'sy'}, use_global_device_ids=true, to_apply=%region_14.15 | all-reduce | flops 2 | bytes 16 | tf_op jit(solution)/shard_map/psum | solution.py:290
  347.6 1.9 collective-permute-start.32
  349.5 4.9 %collective-permute-start.33 = (f32[2,16,1,128]{3,1,2,0:T(8,128)S(1)}, f32[2,16,1,128]{3,1,2,0:T(8,128)S(1)}, u32[]{:S(2)}, u32[]{:S(2)}) collective-permute-start(f32[2,16,1,128]{3,1,2,0:T(8,128)S(1)} %get-tuple-element.101), channel_id=1, source_target_pairs={{8,0},{16,8},{24,16},{32,24},{40,32},{48,40},{56,48},{64,56},{72,6... | collective-permute-start | bytes 49160 | tf_op jit(solution)/shard_map/ppermute | solution.py:21
  355.9 4.0 collective-permute-start.34
  360.0 1.9 collective-permute-start.35
  362.0 2.6 collective-permute-done.34
  364.6 4.0 collective-permute-done.35
  370.1 1.9 collective-permute-start.36
  372.1 4.9 %collective-permute-start.37 = (f32[2,16,1,128]{3,1,2,0:T(8,128)S(1)}, f32[2,16,1,128]{3,1,2,0:T(8,128)S(1)}, u32[]{:S(2)}, u32[]{:S(2)}) collective-permute-start(f32[2,16,1,128]{3,1,2,0:T(8,128)S(1)} %get-tuple-element.99), channel_id=1, source_target_pairs={{8,0},{16,8},{24,16},{32,24},{40,32},{48,40},{56,48},{64,56},{72,6... | collective-permute-start | bytes 49160 | tf_op jit(solution)/shard_map/ppermute | solution.py:21
  378.5 6.1 %collective-permute-start.38 = (f32[2,16,18,1]{3,1,2,0:T(8,128)S(1)}, f32[2,16,18,1]{3,1,2,0:T(8,128)S(1)}, u32[]{:S(2)}, u32[]{:S(2)}) collective-permute-start(f32[2,16,18,1]{3,1,2,0:T(8,128)S(1)} %get-tuple-element.81), channel_id=1, source_target_pairs={{0,1},{1,2},{2,3},{3,4},{4,5},{5,6},{6,7},{8,9},{9,10},{10,11},{11... | collective-permute-start | bytes 6920 | tf_op jit(solution)/shard_map/ppermute | solution.py:19
  384.7 1.9 collective-permute-start.39
  388.9 6.5 %collective-permute-done.39 = f32[2,16,18,1]{3,1,2,0:T(8,128)S(1)} collective-permute-done((f32[2,16,18,1]{3,1,2,0:T(8,128)S(1)}, f32[2,16,18,1]{3,1,2,0:T(8,128)S(1)}, u32[]{:S(2)}, u32[]{:S(2)}) %collective-permute-start.39) | collective-permute-done | bytes 2336 | tf_op jit(solution)/shard_map/ppermute | solution.py:21
  396.9 26.4 %all-reduce.10 = (f32[]{:T(128)}, f32[]{:T(128)}) all-reduce(f32[]{:T(128)} %get-tuple-element.6, f32[]{:T(128)} %get-tuple-element.5), channel_id=1, replica_groups=mesh['section'=2,'sx'=16,'sy'=8] {'sx'}, use_global_device_ids=true, to_apply=%region_19.20 | all-reduce | flops 2 | bytes 16 | tf_op jit(solution)/shard_map/psum | solution.py:291
  423.3 16.5 %all-reduce.14 = (f32[]{:T(128)}, f32[]{:T(128)}) all-reduce(f32[]{:T(128)} %get-tuple-element.13, f32[]{:T(128)} %get-tuple-element.14), channel_id=1, replica_groups=mesh['section'=2,'sx'=16,'sy'=8] {'sy'}, use_global_device_ids=true, to_apply=%region_20.21 | all-reduce | flops 2 | bytes 16 | tf_op jit(solution)/shard_map/psum | solution.py:290
  441.4 8.6 %all_gather.11 = f32[4,16,16,128]{3,2,1,0:T(8,128)S(1)} all-gather(f32[2,16,16,128]{3,2,1,0:T(8,128)S(1)} %copy.346), channel_id=1, replica_groups=mesh['section'=2,'sx'=16,'sy'=8] {'section'}, dimensions={0}, use_global_device_ids=true | all-gather | bytes 786432 | tf_op jit(solution)/shard_map/all_gather | solution.py:296
  (162 shorter events, 55.9 us)
Async XLA Ops:
  0.0 19.2 %copy-start.7 = (f32[16,16,128]{2,1,0:T(8,128)S(1)}, f32[16,16,128]{2,1,0:T(8,128)}, u32[]{:S(2)}) copy-start(f32[16,16,128]{2,1,0:T(8,128)} %param.8) | copy-start | bytes 393220
  0.0 19.2 %copy-start.10 = (f32[16,16,128]{2,1,0:T(8,128)S(1)}, f32[16,16,128]{2,1,0:T(8,128)}, u32[]{:S(2)}) copy-start(f32[16,16,128]{2,1,0:T(8,128)} %param.10) | copy-start | bytes 393220
  0.0 19.2 %copy-start.9 = (f32[16,16,128]{2,1,0:T(8,128)S(1)}, f32[16,16,128]{2,1,0:T(8,128)}, u32[]{:S(2)}) copy-start(f32[16,16,128]{2,1,0:T(8,128)} %param.11) | copy-start | bytes 393220
  1.1 0.7 copy-start.3
  1.8 21.9 %collective-permute-start.4 = (f32[2,16,1,128]{3,1,2,0:T(8,128)S(1)}, f32[2,16,1,128]{3,1,2,0:T(8,128)S(1)}, u32[]{:S(2)}, u32[]{:S(2)}) collective-permute-start(f32[2,16,1,128]{3,1,2,0:T(8,128)S(1)} %get-tuple-element.117), channel_id=1, source_target_pairs={{0,8},{8,16},{16,24},{24,32},{32,40},{40,48},{48,56},{56,64},{64,7... | collective-permute-start | bytes 49160 | tf_op jit(solution)/shard_map/ppermute | solution.py:19
  3.7 27.0 %collective-permute-start.5 = (f32[2,16,1,128]{3,1,2,0:T(8,128)S(1)}, f32[2,16,1,128]{3,1,2,0:T(8,128)S(1)}, u32[]{:S(2)}, u32[]{:S(2)}) collective-permute-start(f32[2,16,1,128]{3,1,2,0:T(8,128)S(1)} %get-tuple-element.116), channel_id=1, source_target_pairs={{8,0},{16,8},{24,16},{32,24},{40,32},{48,40},{56,48},{64,56},{72,6... | collective-permute-start | bytes 49160 | tf_op jit(solution)/shard_map/ppermute | solution.py:21
  10.4 11.6 %copy-start.16 = (f32[2,2]{1,0:T(2,128)S(1)}, f32[2,2]{1,0:T(2,128)}, u32[]{:S(2)}) copy-start(f32[2,2]{1,0:T(2,128)} %constant.39.clone) | copy-start | bytes 52
  10.4 13.4 %copy-start = (f32[2,16,16,128]{3,2,1,0:T(8,128)S(1)}, f32[2,16,16,128]{3,2,1,0:T(8,128)}, u32[]{:S(2)}) copy-start(f32[2,16,16,128]{3,2,1,0:T(8,128)} %param.9) | copy-start | bytes 786436
  23.9 13.5 %collective-permute-start = (f32[4,16,1,128]{3,1,2,0:T(8,128)S(1)}, f32[4,16,1,128]{3,1,2,0:T(8,128)S(1)}, u32[]{:S(2)}, u32[]{:S(2)}) collective-permute-start(f32[4,16,1,128]{3,1,2,0:T(8,128)S(1)} %get-tuple-element.52), channel_id=1, source_target_pairs={{0,8},{8,16},{16,24},{24,32},{32,40},{40,48},{48,56},{56,64},{64,7... | collective-permute-start | bytes 98312 | tf_op jit(solution)/shard_map/ppermute | solution.py:19
  25.8 11.6 %collective-permute-start.1 = (f32[4,16,1,128]{3,1,2,0:T(8,128)S(1)}, f32[4,16,1,128]{3,1,2,0:T(8,128)S(1)}, u32[]{:S(2)}, u32[]{:S(2)}) collective-permute-start(f32[4,16,1,128]{3,1,2,0:T(8,128)S(1)} %get-tuple-element.53), channel_id=1, source_target_pairs={{8,0},{16,8},{24,16},{32,24},{40,32},{48,40},{56,48},{64,56},{72,6... | collective-permute-start | bytes 98312 | tf_op jit(solution)/shard_map/ppermute | solution.py:21
  30.9 13.7 %collective-permute-start.6 = (f32[2,16,18,1]{3,1,2,0:T(8,128)S(1)}, f32[2,16,18,1]{3,1,2,0:T(8,128)}, u32[]{:S(2)}, u32[]{:S(2)}) collective-permute-start(f32[2,16,18,1]{3,1,2,0:T(8,128)S(1)} %get-tuple-element.97), channel_id=1, source_target_pairs={{0,1},{1,2},{2,3},{3,4},{4,5},{5,6},{6,7},{8,9},{9,10},{10,11},{11... | collective-permute-start | bytes 6920 | tf_op jit(solution)/shard_map/ppermute | solution.py:19
  34.3 10.3 %collective-permute-start.7 = (f32[2,16,18,1]{3,1,2,0:T(8,128)S(1)}, f32[2,16,18,1]{3,1,2,0:T(8,128)}, u32[]{:S(2)}, u32[]{:S(2)}) collective-permute-start(f32[2,16,18,1]{3,1,2,0:T(8,128)S(1)} %get-tuple-element.96), channel_id=1, source_target_pairs={{1,0},{2,1},{3,2},{4,3},{5,4},{6,5},{7,6},{9,8},{10,9},{11,10},{12... | collective-permute-start | bytes 6920 | tf_op jit(solution)/shard_map/ppermute | solution.py:21
  38.2 7.8 %collective-permute-start.2 = (f32[4,16,18,1]{2,1,3,0:T(8,128)S(1)}, f32[4,16,18,1]{2,1,3,0:T(8,128)S(1)}, u32[]{:S(2)}, u32[]{:S(2)}) collective-permute-start(f32[4,16,18,1]{2,1,3,0:T(8,128)S(1)} %copy.321), channel_id=1, source_target_pairs={{0,1},{1,2},{2,3},{3,4},{4,5},{5,6},{6,7},{8,9},{9,10},{10,11},{11... | collective-permute-start | bytes 13832 | tf_op jit(solution)/shard_map/ppermute | solution.py:19
  41.4 5.9 %collective-permute-start.3 = (f32[4,16,18,1]{2,1,3,0:T(8,128)S(1)}, f32[4,16,18,1]{2,1,3,0:T(8,128)}, u32[]{:S(2)}, u32[]{:S(2)}) collective-permute-start(f32[4,16,18,1]{2,1,3,0:T(8,128)S(1)} %copy.322), channel_id=1, source_target_pairs={{1,0},{2,1},{3,2},{4,3},{5,4},{6,5},{7,6},{9,8},{10,9},{11,10},{12... | collective-permute-start | bytes 13832 | tf_op jit(solution)/shard_map/ppermute | solution.py:21
  49.4 1.0 copy-start.4
  49.4 1.0 copy-start.8
  52.2 9.0 %copy-start.1 = (f32[16,16,128]{2,0,1:T(8,128)S(1)}, f32[16,16,128]{2,0,1:T(8,128)}, u32[]{:S(2)}) copy-start(f32[16,16,128]{2,0,1:T(8,128)} %copy.344) | copy-start | bytes 393220
  52.2 9.0 %copy-start.2 = (f32[16,16,128]{2,0,1:T(8,128)S(1)}, f32[16,16,128]{2,0,1:T(8,128)}, u32[]{:S(2)}) copy-start(f32[16,16,128]{2,0,1:T(8,128)} %copy.345) | copy-start | bytes 393220
  52.2 9.0 %copy-start.11 = (f32[2]{0:T(128)S(1)}, f32[2]{0:T(128)}, u32[]{:S(2)}) copy-start(f32[2]{0:T(128)} %get-tuple-element.130) | copy-start | bytes 28
  52.3 9.0 %copy-start.12 = (f32[2]{0:T(128)S(1)}, f32[2]{0:T(128)}, u32[]{:S(2)}) copy-start(f32[2]{0:T(128)} %get-tuple-element.131) | copy-start | bytes 28
  52.3 9.0 %copy-start.13 = (f32[2]{0:T(128)S(1)}, f32[2]{0:T(128)}, u32[]{:S(2)}) copy-start(f32[2]{0:T(128)} %get-tuple-element.132) | copy-start | bytes 28
  52.3 9.0 %copy-start.14 = (f32[2]{0:T(128)S(1)}, f32[2]{0:T(128)}, u32[]{:S(2)}) copy-start(f32[2]{0:T(128)} %get-tuple-element.133) | copy-start | bytes 28
  63.6 6.8 %collective-permute-start.8 = (f32[2,16,1,128]{3,1,2,0:T(8,128)S(1)}, f32[2,16,1,128]{3,1,2,0:T(8,128)S(1)}, u32[]{:S(2)}, u32[]{:S(2)}) collective-permute-start(f32[2,16,1,128]{3,1,2,0:T(8,128)S(1)} %get-tuple-element.112), channel_id=1, source_target_pairs={{0,8},{8,16},{16,24},{24,32},{32,40},{40,48},{48,56},{56,64},{64,7... | collective-permute-start | bytes 49160 | tf_op jit(solution)/shard_map/ppermute | solution.py:19
  65.5 6.3 %collective-permute-start.9 = (f32[2,16,1,128]{3,1,2,0:T(8,128)S(1)}, f32[2,16,1,128]{3,1,2,0:T(8,128)S(1)}, u32[]{:S(2)}, u32[]{:S(2)}) collective-permute-start(f32[2,16,1,128]{3,1,2,0:T(8,128)S(1)} %get-tuple-element.113), channel_id=1, source_target_pairs={{8,0},{16,8},{24,16},{32,24},{40,32},{48,40},{56,48},{64,56},{72,6... | collective-permute-start | bytes 49160 | tf_op jit(solution)/shard_map/ppermute | solution.py:21
  71.9 9.8 %collective-permute-start.10 = (f32[2,16,18,1]{3,1,2,0:T(8,128)S(1)}, f32[2,16,18,1]{3,1,2,0:T(8,128)S(1)}, u32[]{:S(2)}, u32[]{:S(2)}) collective-permute-start(f32[2,16,18,1]{3,1,2,0:T(8,128)S(1)} %get-tuple-element.95), channel_id=1, source_target_pairs={{0,1},{1,2},{2,3},{3,4},{4,5},{5,6},{6,7},{8,9},{9,10},{10,11},{11... | collective-permute-start | bytes 6920 | tf_op jit(solution)/shard_map/ppermute | solution.py:19
  76.7 11.6 %collective-permute-start.11 = (f32[2,16,18,1]{3,1,2,0:T(8,128)S(1)}, f32[2,16,18,1]{3,1,2,0:T(8,128)S(1)}, u32[]{:S(2)}, u32[]{:S(2)}) collective-permute-start(f32[2,16,18,1]{3,1,2,0:T(8,128)S(1)} %get-tuple-element.94), channel_id=1, source_target_pairs={{1,0},{2,1},{3,2},{4,3},{5,4},{6,5},{7,6},{9,8},{10,9},{11,10},{12... | collective-permute-start | bytes 6920 | tf_op jit(solution)/shard_map/ppermute | solution.py:21
  89.7 8.5 %copy-start.5 = (f32[1,16,16,128]{3,1,2,0:T(8,128)}, f32[1,16,16,128]{3,1,2,0:T(8,128)S(1)}, u32[]{:S(2)}) copy-start(f32[1,16,16,128]{3,1,2,0:T(8,128)S(1)} %get-tuple-element.79) | copy-start | bytes 393220
  89.8 6.8 %collective-permute-start.12 = (f32[2,16,1,128]{3,1,2,0:T(8,128)S(1)}, f32[2,16,1,128]{3,1,2,0:T(8,128)S(1)}, u32[]{:S(2)}, u32[]{:S(2)}) collective-permute-start(f32[2,16,1,128]{3,1,2,0:T(8,128)S(1)} %get-tuple-element.110), channel_id=1, source_target_pairs={{0,8},{8,16},{16,24},{24,32},{32,40},{40,48},{48,56},{56,64},{64,7... | collective-permute-start | bytes 49160 | tf_op jit(solution)/shard_map/ppermute | solution.py:19
  91.7 6.3 %collective-permute-start.13 = (f32[2,16,1,128]{3,1,2,0:T(8,128)S(1)}, f32[2,16,1,128]{3,1,2,0:T(8,128)S(1)}, u32[]{:S(2)}, u32[]{:S(2)}) collective-permute-start(f32[2,16,1,128]{3,1,2,0:T(8,128)S(1)} %get-tuple-element.111), channel_id=1, source_target_pairs={{8,0},{16,8},{24,16},{32,24},{40,32},{48,40},{56,48},{64,56},{72,6... | collective-permute-start | bytes 49160 | tf_op jit(solution)/shard_map/ppermute | solution.py:21
  98.2 10.4 %collective-permute-start.14 = (f32[2,16,18,1]{3,1,2,0:T(8,128)S(1)}, f32[2,16,18,1]{3,1,2,0:T(8,128)S(1)}, u32[]{:S(2)}, u32[]{:S(2)}) collective-permute-start(f32[2,16,18,1]{3,1,2,0:T(8,128)S(1)} %get-tuple-element.93), channel_id=1, source_target_pairs={{0,1},{1,2},{2,3},{3,4},{4,5},{5,6},{6,7},{8,9},{9,10},{10,11},{11... | collective-permute-start | bytes 6920 | tf_op jit(solution)/shard_map/ppermute | solution.py:19
  101.9 11.1 %collective-permute-start.15 = (f32[2,16,18,1]{3,1,2,0:T(8,128)S(1)}, f32[2,16,18,1]{3,1,2,0:T(8,128)S(1)}, u32[]{:S(2)}, u32[]{:S(2)}) collective-permute-start(f32[2,16,18,1]{3,1,2,0:T(8,128)S(1)} %get-tuple-element.92), channel_id=1, source_target_pairs={{1,0},{2,1},{3,2},{4,3},{5,4},{6,5},{7,6},{9,8},{10,9},{11,10},{12... | collective-permute-start | bytes 6920 | tf_op jit(solution)/shard_map/ppermute | solution.py:21
  159.1 6.8 %collective-permute-start.16 = (f32[2,16,1,128]{3,1,2,0:T(8,128)S(1)}, f32[2,16,1,128]{3,1,2,0:T(8,128)S(1)}, u32[]{:S(2)}, u32[]{:S(2)}) collective-permute-start(f32[2,16,1,128]{3,1,2,0:T(8,128)S(1)} %get-tuple-element.108), channel_id=1, source_target_pairs={{0,8},{8,16},{16,24},{24,32},{32,40},{40,48},{48,56},{56,64},{64,7... | collective-permute-start | bytes 49160 | tf_op jit(solution)/shard_map/ppermute | solution.py:19
  161.0 6.3 %collective-permute-start.17 = (f32[2,16,1,128]{3,1,2,0:T(8,128)S(1)}, f32[2,16,1,128]{3,1,2,0:T(8,128)S(1)}, u32[]{:S(2)}, u32[]{:S(2)}) collective-permute-start(f32[2,16,1,128]{3,1,2,0:T(8,128)S(1)} %get-tuple-element.109), channel_id=1, source_target_pairs={{8,0},{16,8},{24,16},{32,24},{40,32},{48,40},{56,48},{64,56},{72,6... | collective-permute-start | bytes 49160 | tf_op jit(solution)/shard_map/ppermute | solution.py:21
  167.5 8.6 %collective-permute-start.18 = (f32[2,16,18,1]{3,1,2,0:T(8,128)S(1)}, f32[2,16,18,1]{3,1,2,0:T(8,128)S(1)}, u32[]{:S(2)}, u32[]{:S(2)}) collective-permute-start(f32[2,16,18,1]{3,1,2,0:T(8,128)S(1)} %get-tuple-element.91), channel_id=1, source_target_pairs={{0,1},{1,2},{2,3},{3,4},{4,5},{5,6},{6,7},{8,9},{9,10},{10,11},{11... | collective-permute-start | bytes 6920 | tf_op jit(solution)/shard_map/ppermute | solution.py:19
  171.5 8.6 %collective-permute-start.19 = (f32[2,16,18,1]{3,1,2,0:T(8,128)S(1)}, f32[2,16,18,1]{3,1,2,0:T(8,128)S(1)}, u32[]{:S(2)}, u32[]{:S(2)}) collective-permute-start(f32[2,16,18,1]{3,1,2,0:T(8,128)S(1)} %get-tuple-element.90), channel_id=1, source_target_pairs={{1,0},{2,1},{3,2},{4,3},{5,4},{6,5},{7,6},{9,8},{10,9},{11,10},{12... | collective-permute-start | bytes 6920 | tf_op jit(solution)/shard_map/ppermute | solution.py:21
  181.7 6.8 %collective-permute-start.20 = (f32[2,16,1,128]{3,1,2,0:T(8,128)S(1)}, f32[2,16,1,128]{3,1,2,0:T(8,128)S(1)}, u32[]{:S(2)}, u32[]{:S(2)}) collective-permute-start(f32[2,16,1,128]{3,1,2,0:T(8,128)S(1)} %get-tuple-element.106), channel_id=1, source_target_pairs={{0,8},{8,16},{16,24},{24,32},{32,40},{40,48},{48,56},{56,64},{64,7... | collective-permute-start | bytes 49160 | tf_op jit(solution)/shard_map/ppermute | solution.py:19
  183.6 6.3 %collective-permute-start.21 = (f32[2,16,1,128]{3,1,2,0:T(8,128)S(1)}, f32[2,16,1,128]{3,1,2,0:T(8,128)S(1)}, u32[]{:S(2)}, u32[]{:S(2)}) collective-permute-start(f32[2,16,1,128]{3,1,2,0:T(8,128)S(1)} %get-tuple-element.107), channel_id=1, source_target_pairs={{8,0},{16,8},{24,16},{32,24},{40,32},{48,40},{56,48},{64,56},{72,6... | collective-permute-start | bytes 49160 | tf_op jit(solution)/shard_map/ppermute | solution.py:21
  190.1 10.4 %collective-permute-start.22 = (f32[2,16,18,1]{3,1,2,0:T(8,128)S(1)}, f32[2,16,18,1]{3,1,2,0:T(8,128)S(1)}, u32[]{:S(2)}, u32[]{:S(2)}) collective-permute-start(f32[2,16,18,1]{3,1,2,0:T(8,128)S(1)} %get-tuple-element.89), channel_id=1, source_target_pairs={{0,1},{1,2},{2,3},{3,4},{4,5},{5,6},{6,7},{8,9},{9,10},{10,11},{11... | collective-permute-start | bytes 6920 | tf_op jit(solution)/shard_map/ppermute | solution.py:19
  196.2 10.7 %collective-permute-start.23 = (f32[2,16,18,1]{3,1,2,0:T(8,128)S(1)}, f32[2,16,18,1]{3,1,2,0:T(8,128)S(1)}, u32[]{:S(2)}, u32[]{:S(2)}) collective-permute-start(f32[2,16,18,1]{3,1,2,0:T(8,128)S(1)} %get-tuple-element.88), channel_id=1, source_target_pairs={{1,0},{2,1},{3,2},{4,3},{5,4},{6,5},{7,6},{9,8},{10,9},{11,10},{12... | collective-permute-start | bytes 6920 | tf_op jit(solution)/shard_map/ppermute | solution.py:21
  253.3 6.8 %collective-permute-start.24 = (f32[2,16,1,128]{3,1,2,0:T(8,128)S(1)}, f32[2,16,1,128]{3,1,2,0:T(8,128)S(1)}, u32[]{:S(2)}, u32[]{:S(2)}) collective-permute-start(f32[2,16,1,128]{3,1,2,0:T(8,128)S(1)} %get-tuple-element.104), channel_id=1, source_target_pairs={{0,8},{8,16},{16,24},{24,32},{32,40},{40,48},{48,56},{56,64},{64,7... | collective-permute-start | bytes 49160 | tf_op jit(solution)/shard_map/ppermute | solution.py:19
  255.3 6.3 %collective-permute-start.25 = (f32[2,16,1,128]{3,1,2,0:T(8,128)S(1)}, f32[2,16,1,128]{3,1,2,0:T(8,128)S(1)}, u32[]{:S(2)}, u32[]{:S(2)}) collective-permute-start(f32[2,16,1,128]{3,1,2,0:T(8,128)S(1)} %get-tuple-element.105), channel_id=1, source_target_pairs={{8,0},{16,8},{24,16},{32,24},{40,32},{48,40},{56,48},{64,56},{72,6... | collective-permute-start | bytes 49160 | tf_op jit(solution)/shard_map/ppermute | solution.py:21
  261.7 8.6 %collective-permute-start.26 = (f32[2,16,18,1]{3,1,2,0:T(8,128)S(1)}, f32[2,16,18,1]{3,1,2,0:T(8,128)S(1)}, u32[]{:S(2)}, u32[]{:S(2)}) collective-permute-start(f32[2,16,18,1]{3,1,2,0:T(8,128)S(1)} %get-tuple-element.87), channel_id=1, source_target_pairs={{0,1},{1,2},{2,3},{3,4},{4,5},{5,6},{6,7},{8,9},{9,10},{10,11},{11... | collective-permute-start | bytes 6920 | tf_op jit(solution)/shard_map/ppermute | solution.py:19
  265.8 8.6 %collective-permute-start.27 = (f32[2,16,18,1]{3,1,2,0:T(8,128)S(1)}, f32[2,16,18,1]{3,1,2,0:T(8,128)S(1)}, u32[]{:S(2)}, u32[]{:S(2)}) collective-permute-start(f32[2,16,18,1]{3,1,2,0:T(8,128)S(1)} %get-tuple-element.86), channel_id=1, source_target_pairs={{1,0},{2,1},{3,2},{4,3},{5,4},{6,5},{7,6},{9,8},{10,9},{11,10},{12... | collective-permute-start | bytes 6920 | tf_op jit(solution)/shard_map/ppermute | solution.py:21
  275.9 6.8 %collective-permute-start.28 = (f32[2,16,1,128]{3,1,2,0:T(8,128)S(1)}, f32[2,16,1,128]{3,1,2,0:T(8,128)S(1)}, u32[]{:S(2)}, u32[]{:S(2)}) collective-permute-start(f32[2,16,1,128]{3,1,2,0:T(8,128)S(1)} %get-tuple-element.102), channel_id=1, source_target_pairs={{0,8},{8,16},{16,24},{24,32},{32,40},{40,48},{48,56},{56,64},{64,7... | collective-permute-start | bytes 49160 | tf_op jit(solution)/shard_map/ppermute | solution.py:19
  277.8 6.3 %collective-permute-start.29 = (f32[2,16,1,128]{3,1,2,0:T(8,128)S(1)}, f32[2,16,1,128]{3,1,2,0:T(8,128)S(1)}, u32[]{:S(2)}, u32[]{:S(2)}) collective-permute-start(f32[2,16,1,128]{3,1,2,0:T(8,128)S(1)} %get-tuple-element.103), channel_id=1, source_target_pairs={{8,0},{16,8},{24,16},{32,24},{40,32},{48,40},{56,48},{64,56},{72,6... | collective-permute-start | bytes 49160 | tf_op jit(solution)/shard_map/ppermute | solution.py:21
  284.3 10.4 %collective-permute-start.30 = (f32[2,16,18,1]{3,1,2,0:T(8,128)S(1)}, f32[2,16,18,1]{3,1,2,0:T(8,128)S(1)}, u32[]{:S(2)}, u32[]{:S(2)}) collective-permute-start(f32[2,16,18,1]{3,1,2,0:T(8,128)S(1)} %get-tuple-element.85), channel_id=1, source_target_pairs={{0,1},{1,2},{2,3},{3,4},{4,5},{5,6},{6,7},{8,9},{9,10},{10,11},{11... | collective-permute-start | bytes 6920 | tf_op jit(solution)/shard_map/ppermute | solution.py:19
  290.4 10.7 %collective-permute-start.31 = (f32[2,16,18,1]{3,1,2,0:T(8,128)S(1)}, f32[2,16,18,1]{3,1,2,0:T(8,128)S(1)}, u32[]{:S(2)}, u32[]{:S(2)}) collective-permute-start(f32[2,16,18,1]{3,1,2,0:T(8,128)S(1)} %get-tuple-element.84), channel_id=1, source_target_pairs={{1,0},{2,1},{3,2},{4,3},{5,4},{6,5},{7,6},{9,8},{10,9},{11,10},{12... | collective-permute-start | bytes 6920 | tf_op jit(solution)/shard_map/ppermute | solution.py:21
  302.7 59.2 %copy-start.15 = (f32[4,4]{0,1:T(4,128)S(1)}, f32[4,4]{0,1:T(4,128)}, u32[]{:S(2)}) copy-start(f32[4,4]{0,1:T(4,128)} %constant.38.clone) | copy-start | bytes 196
  347.6 6.8 %collective-permute-start.32 = (f32[2,16,1,128]{3,1,2,0:T(8,128)S(1)}, f32[2,16,1,128]{3,1,2,0:T(8,128)S(1)}, u32[]{:S(2)}, u32[]{:S(2)}) collective-permute-start(f32[2,16,1,128]{3,1,2,0:T(8,128)S(1)} %get-tuple-element.100), channel_id=1, source_target_pairs={{0,8},{8,16},{16,24},{24,32},{32,40},{40,48},{48,56},{56,64},{64,7... | collective-permute-start | bytes 49160 | tf_op jit(solution)/shard_map/ppermute | solution.py:19
  349.5 6.3 %collective-permute-start.33 = (f32[2,16,1,128]{3,1,2,0:T(8,128)S(1)}, f32[2,16,1,128]{3,1,2,0:T(8,128)S(1)}, u32[]{:S(2)}, u32[]{:S(2)}) collective-permute-start(f32[2,16,1,128]{3,1,2,0:T(8,128)S(1)} %get-tuple-element.101), channel_id=1, source_target_pairs={{8,0},{16,8},{24,16},{32,24},{40,32},{48,40},{56,48},{64,56},{72,6... | collective-permute-start | bytes 49160 | tf_op jit(solution)/shard_map/ppermute | solution.py:21
  355.9 8.6 %collective-permute-start.34 = (f32[2,16,18,1]{3,1,2,0:T(8,128)S(1)}, f32[2,16,18,1]{3,1,2,0:T(8,128)S(1)}, u32[]{:S(2)}, u32[]{:S(2)}) collective-permute-start(f32[2,16,18,1]{3,1,2,0:T(8,128)S(1)} %get-tuple-element.83), channel_id=1, source_target_pairs={{0,1},{1,2},{2,3},{3,4},{4,5},{5,6},{6,7},{8,9},{9,10},{10,11},{11... | collective-permute-start | bytes 6920 | tf_op jit(solution)/shard_map/ppermute | solution.py:19
  360.0 8.6 %collective-permute-start.35 = (f32[2,16,18,1]{3,1,2,0:T(8,128)S(1)}, f32[2,16,18,1]{3,1,2,0:T(8,128)S(1)}, u32[]{:S(2)}, u32[]{:S(2)}) collective-permute-start(f32[2,16,18,1]{3,1,2,0:T(8,128)S(1)} %get-tuple-element.82), channel_id=1, source_target_pairs={{1,0},{2,1},{3,2},{4,3},{5,4},{6,5},{7,6},{9,8},{10,9},{11,10},{12... | collective-permute-start | bytes 6920 | tf_op jit(solution)/shard_map/ppermute | solution.py:21
  370.1 6.8 %collective-permute-start.36 = (f32[2,16,1,128]{3,1,2,0:T(8,128)S(1)}, f32[2,16,1,128]{3,1,2,0:T(8,128)S(1)}, u32[]{:S(2)}, u32[]{:S(2)}) collective-permute-start(f32[2,16,1,128]{3,1,2,0:T(8,128)S(1)} %get-tuple-element.98), channel_id=1, source_target_pairs={{0,8},{8,16},{16,24},{24,32},{32,40},{40,48},{48,56},{56,64},{64,7... | collective-permute-start | bytes 49160 | tf_op jit(solution)/shard_map/ppermute | solution.py:19
  372.1 6.3 %collective-permute-start.37 = (f32[2,16,1,128]{3,1,2,0:T(8,128)S(1)}, f32[2,16,1,128]{3,1,2,0:T(8,128)S(1)}, u32[]{:S(2)}, u32[]{:S(2)}) collective-permute-start(f32[2,16,1,128]{3,1,2,0:T(8,128)S(1)} %get-tuple-element.99), channel_id=1, source_target_pairs={{8,0},{16,8},{24,16},{32,24},{40,32},{48,40},{56,48},{64,56},{72,6... | collective-permute-start | bytes 49160 | tf_op jit(solution)/shard_map/ppermute | solution.py:21
  378.5 10.4 %collective-permute-start.38 = (f32[2,16,18,1]{3,1,2,0:T(8,128)S(1)}, f32[2,16,18,1]{3,1,2,0:T(8,128)S(1)}, u32[]{:S(2)}, u32[]{:S(2)}) collective-permute-start(f32[2,16,18,1]{3,1,2,0:T(8,128)S(1)} %get-tuple-element.81), channel_id=1, source_target_pairs={{0,1},{1,2},{2,3},{3,4},{4,5},{5,6},{6,7},{8,9},{9,10},{10,11},{11... | collective-permute-start | bytes 6920 | tf_op jit(solution)/shard_map/ppermute | solution.py:19
  384.7 10.7 %collective-permute-start.39 = (f32[2,16,18,1]{3,1,2,0:T(8,128)S(1)}, f32[2,16,18,1]{3,1,2,0:T(8,128)S(1)}, u32[]{:S(2)}, u32[]{:S(2)}) collective-permute-start(f32[2,16,18,1]{3,1,2,0:T(8,128)S(1)} %get-tuple-element.80), channel_id=1, source_target_pairs={{1,0},{2,1},{3,2},{4,3},{5,4},{6,5},{7,6},{9,8},{10,9},{11,10},{12... | collective-permute-start | bytes 6920 | tf_op jit(solution)/shard_map/ppermute | solution.py:21
  395.8 45.3 %copy-start.6 = (f32[1,16,16,128]{3,1,2,0:T(8,128)S(1)}, f32[1,16,16,128]{3,1,2,0:T(8,128)}, u32[]{:S(2)}) copy-start(f32[1,16,16,128]{3,1,2,0:T(8,128)} %copy-done.5) | copy-start | bytes 393220
